TPU v7x, 512 devices: a whole 4x4x16 slice. The times are simulated.
512 devices in a mesh: row: 16 (over z_lo, core), col: 4 (over x), layer: 8 (over y, z_hi).
Axes of the slice: x: 4, y: 4, z: 16 (z_hi: 2, z_lo: 8; z = z_hi * 8 + z_lo), core: 2. Of those that a mesh axis runs over, the one named last changes fastest.
Arguments:
- density: bfloat16 [1024, 11, 128, 128], P(('row', 'layer'), None, 'col'), may hold values from -1.5 to 1.5, as said below
- pattern: int32 [1024, 11], replicated, may hold values from -1 to 1023, as said below
- square_filter: int32 [1024, 12], replicated, may hold values from 0 to 1023, as said below
- cube_filter: int32 [1024, 16], replicated, may hold values from 0 to 1023, as said below
Outputs:
- purified: float32 [1024, 16, 128, 128], P(('row', 'layer'), 'col')
Inputs may be any that keep to these rules, and one draw needn't show every extreme that they name: `density`: slot s of block row i holds the block of P at (i, pattern[i, s]), and zeros where pattern[i, s] is -1; the matrix so described is exactly symmetric. Row i lists distinct block columns, each within 5 of i modulo 1024, i itself among them; unused slots hold -1; the block pattern is symmetric; some block row uses all 11 slots. `square_filter`: row i lists 12 distinct block columns, each within 10 of i modulo 1024. `cube_filter`: row i lists 16 distinct block columns, each within 15 of i modulo 1024.
All inputs are finite; a program needn't handle non-finite values.
Results may differ from a plain program's by a relative error of at most 0.0023.
Values may be sent and summed in bfloat16 or wider, within the bound.
A program may use at most 64 MiB of HBM per device.

v0:
```python
import jax
import jax.numpy as jnp
from jax import lax
from jax.sharding import PartitionSpec as P

RADIUS = 5


def extended_2(x, sides, width):
    for axis, dim in sides:
        size, length = (lax.axis_size(axis), x.shape[dim])
        up = [(i, (i + 1) % size) for i in range(size)]
        down = [(j, i) for i, j in up]
        last = lax.slice_in_dim(x, length - width, length, axis=dim)
        leading = lax.slice_in_dim(x, 0, width, axis=dim)
        before = lax.ppermute(last, axis, up)
        after = lax.ppermute(leading, axis, down)
        x = jnp.concatenate([before, x, after], axis=dim)
    return x


def matched_slots(listed, targets):
    match = listed[:, None, :] == targets[None, :, None]
    slot_ids = jnp.arange(listed.shape[1], dtype=jnp.int32)
    picked_slot = jnp.sum(jnp.where(match, slot_ids[None, None, :], 0), axis=2)
    return (picked_slot, jnp.any(match, axis=2))


def per_device(density, pattern, square_filter, cube_filter):
    layer_count = lax.axis_size("layer")
    stack_count = lax.axis_size("row") * layer_count
    col_count = lax.axis_size("col")
    col_index = lax.axis_index("col")
    local_rows = density.shape[0]
    total_rows = local_rows * stack_count
    first_row = (lax.axis_index("row") * layer_count + lax.axis_index("layer")) * local_rows
    rows_iota = jnp.arange(local_rows, dtype=jnp.int32)
    whole_rows = lax.all_gather(density, "col", axis=2, tiled=True)
    extended = extended_2(whole_rows, ((("row", "layer"), 0),), RADIUS)

    def product_row(local_row, right_blocks, right_lists, targets):
        global_row = first_row + local_row
        listed = lax.dynamic_index_in_dim(pattern, global_row, 0, keepdims=False)
        source = jnp.where(listed >= 0, listed, global_row)
        offset = (source - global_row + RADIUS + total_rows) % total_rows - RADIUS
        position = local_row + RADIUS + offset
        right_listed = jnp.take(right_lists, source, axis=0)
        picked_slot, found = matched_slots(right_listed, targets)
        picked = right_blocks[position[:, None], picked_slot]
        picked = jnp.where(found[:, :, None, None], picked, jnp.zeros((), picked.dtype))
        left = extended[local_row + RADIUS]
        return jnp.einsum("axy,ajyz->jxz", left, picked, preferred_element_type=jnp.float32)

    def square_whole(local_row):
        targets = lax.dynamic_index_in_dim(square_filter, first_row + local_row, 0, keepdims=False)
        return product_row(local_row, extended, pattern, targets).astype(jnp.bfloat16)

    square_full = lax.map(square_whole, rows_iota)
    square_ext = extended_2(square_full, ((("row", "layer"), 0),), RADIUS)
    cube_share = cube_filter.shape[1] // col_count

    def purified_row(local_row):
        global_row = first_row + local_row
        row_cube = lax.dynamic_index_in_dim(cube_filter, global_row, 0, keepdims=False)
        targets = lax.dynamic_slice_in_dim(row_cube, col_index * cube_share, cube_share, 0)
        cube = product_row(local_row, square_ext, square_filter, targets)
        own_filter = lax.dynamic_index_in_dim(square_filter, global_row, 0, keepdims=False)
        chooser = (targets[:, None] == own_filter[None, :]).astype(jnp.bfloat16)
        own_square = jnp.einsum(
            "tj,jxz->txz",
            chooser,
            square_ext[local_row + RADIUS],
            preferred_element_type=jnp.float32,
        )
        return 3.0 * own_square - 2.0 * cube

    return lax.map(purified_row, rows_iota)


def solution(mesh):
    in_specs = (P(("row", "layer"), None, "col", None), P(), P(), P())
    out_specs = P(("row", "layer"), "col", None, None)
    return jax.shard_map(
        per_device, mesh=mesh, in_specs=in_specs, out_specs=out_specs, check_vma=False
    )
```

profile of v0, /device:TPU:32, one launch (start us, length us, event | category | flops | bytes accessed | tf_op | source)
XLA Modules:
  0.0 1217.8 jit_solution(2940762611072111093)
XLA Ops:
  7.3 51.3 %all-gather.2.cloned.1.call-done = bf16[8,11,128,128]{3,2,1,0:T(8,128)(2,1)} async-done(((bf16[8,11,32,128]{3,2,1,0:T(8,128)(2,1)}), bf16[8,11,128,128]{3,2,1,0:T(8,128)(2,1)}) %all-gather.2.cloned.1.call-update) | async-done | bytes 2883600 | tf_op jit(solution)/shard_map/all_gather | solution.py:38
  63.0 11.9 collective-permute-start
  80.6 364.5 %collective-permute-done = bf16[5,11,128,128]{3,2,1,0:T(8,128)(2,1)} collective-permute-done((bf16[5,11,128,128]{3,2,1,0:T(8,128)(2,1)}, bf16[5,11,128,128]{3,2,1,0:T(8,128)(2,1)}, u32[]{:S(2)}, u32[]{:S(2)}) %collective-permute-start) | collective-permute-done | bytes 1802272 | tf_op jit(solution)/shard_map/ppermute | solution.py:16
  451.6 281.2 %while.25 = (s32[]{:T(128)}, bf16[8,12,128,128]{3,2,1,0:T(8,128)(2,1)S(1)}, s32[8]{0:T(128)S(1)}, s32[]{:T(128)}, s32[1024,11]{1,0:T(8,128)}, /*index=5*/s32[102...) while((s32[]{:T(128)}, ...), condition=%wide.region_3.4_spmd, body=%wide.region_0.3_spmd.sunk | while | flops 556016768 | bytes 23965456 | solution.py:58
  458.5 15.0 %gather_fusion.1 = bf16[132,128,128]{2,1,0:T(8,128)(2,1)} fusion(bf16[18,11,128,128]{3,2,1,0:T(8,128)(2,1)} %get-tuple-element.525, s32[132]{0:T(256)S(1)} %reshape.262), kind=kCustom, calls=%fused_computation.1.clone.1 | custom fusion | bytes 8651808 | tf_op jit(solution)/shard_map/while/body/eval_jaxpr/gather | solution.py:49
  473.5 6.5 copy.83
  481.1 4.4 fusion.97
  493.6 15.0 %gather_fusion.1 = bf16[132,128,128]{2,1,0:T(8,128)(2,1)} fusion(bf16[18,11,128,128]{3,2,1,0:T(8,128)(2,1)} %get-tuple-element.525, s32[132]{0:T(256)S(1)} %reshape.262), kind=kCustom, calls=%fused_computation.1.clone.1 | custom fusion | bytes 8651808 | tf_op jit(solution)/shard_map/while/body/eval_jaxpr/gather | solution.py:49
  508.6 6.5 copy.83
  516.2 4.4 fusion.97
  528.8 15.0 %gather_fusion.1 = bf16[132,128,128]{2,1,0:T(8,128)(2,1)} fusion(bf16[18,11,128,128]{3,2,1,0:T(8,128)(2,1)} %get-tuple-element.525, s32[132]{0:T(256)S(1)} %reshape.262), kind=kCustom, calls=%fused_computation.1.clone.1 | custom fusion | bytes 8651808 | tf_op jit(solution)/shard_map/while/body/eval_jaxpr/gather | solution.py:49
  543.8 6.5 copy.83
  551.4 4.4 fusion.97
  564.0 15.0 %gather_fusion.1 = bf16[132,128,128]{2,1,0:T(8,128)(2,1)} fusion(bf16[18,11,128,128]{3,2,1,0:T(8,128)(2,1)} %get-tuple-element.525, s32[132]{0:T(256)S(1)} %reshape.262), kind=kCustom, calls=%fused_computation.1.clone.1 | custom fusion | bytes 8651808 | tf_op jit(solution)/shard_map/while/body/eval_jaxpr/gather | solution.py:49
  579.0 6.5 copy.83
  586.5 4.4 fusion.97
  599.1 15.0 %gather_fusion.1 = bf16[132,128,128]{2,1,0:T(8,128)(2,1)} fusion(bf16[18,11,128,128]{3,2,1,0:T(8,128)(2,1)} %get-tuple-element.525, s32[132]{0:T(256)S(1)} %reshape.262), kind=kCustom, calls=%fused_computation.1.clone.1 | custom fusion | bytes 8651808 | tf_op jit(solution)/shard_map/while/body/eval_jaxpr/gather | solution.py:49
  614.1 6.5 copy.83
  621.7 4.4 fusion.97
  634.3 15.0 %gather_fusion.1 = bf16[132,128,128]{2,1,0:T(8,128)(2,1)} fusion(bf16[18,11,128,128]{3,2,1,0:T(8,128)(2,1)} %get-tuple-element.525, s32[132]{0:T(256)S(1)} %reshape.262), kind=kCustom, calls=%fused_computation.1.clone.1 | custom fusion | bytes 8651808 | tf_op jit(solution)/shard_map/while/body/eval_jaxpr/gather | solution.py:49
  649.3 6.5 copy.83
  656.9 4.4 fusion.97
  669.4 15.0 %gather_fusion.1 = bf16[132,128,128]{2,1,0:T(8,128)(2,1)} fusion(bf16[18,11,128,128]{3,2,1,0:T(8,128)(2,1)} %get-tuple-element.525, s32[132]{0:T(256)S(1)} %reshape.262), kind=kCustom, calls=%fused_computation.1.clone.1 | custom fusion | bytes 8651808 | tf_op jit(solution)/shard_map/while/body/eval_jaxpr/gather | solution.py:49
  684.4 6.5 copy.83
  692.0 4.4 fusion.97
  704.6 15.0 %gather_fusion.1 = bf16[132,128,128]{2,1,0:T(8,128)(2,1)} fusion(bf16[18,11,128,128]{3,2,1,0:T(8,128)(2,1)} %get-tuple-element.525, s32[132]{0:T(256)S(1)} %reshape.262), kind=kCustom, calls=%fused_computation.1.clone.1 | custom fusion | bytes 8651808 | tf_op jit(solution)/shard_map/while/body/eval_jaxpr/gather | solution.py:49
  719.6 6.5 copy.83
  727.2 4.4 fusion.97
  737.3 13.6 %collective-permute-start.3 = (bf16[5,12,128,128]{3,2,1,0:T(8,128)(2,1)}, bf16[5,12,128,128]{3,2,1,0:T(8,128)(2,1)}, u32[]{:S(2)}, u32[]{:S(2)}) collective-permute-start(bf16[5,12,128,128]{3,2,1,0:T(8,128)(2,1)} %get-tuple-element.388), channel_id=1, source_target_pairs={{1,0},{2,1},{3,2},{4,3},{5,4},{6,5},{7,6},{32,7},{33,32},{34,33},{... | collective-permute-start | bytes 5898248 | tf_op jit(solution)/shard_map/ppermute | solution.py:17
  752.0 315.7 %collective-permute-done.2 = bf16[5,12,128,128]{3,2,1,0:T(8,128)(2,1)} collective-permute-done((bf16[5,12,128,128]{3,2,1,0:T(8,128)(2,1)}, bf16[5,12,128,128]{3,2,1,0:T(8,128)(2,1)}, u32[]{:S(2)}, u32[]{:S(2)}) %collective-permute-start.2) | collective-permute-done | bytes 1966112 | tf_op jit(solution)/shard_map/ppermute | solution.py:16
  1067.6 5.6 pad_maximum_fusion
  1073.3 137.6 %while.26 = (s32[]{:T(128)}, f32[8,4,128,128]{3,2,1,0:T(8,128)}, s32[8]{0:T(128)S(1)}, s32[]{:T(128)}, s32[1024,16]{1,0:T(8,128)}, /*index=5*/s32[]{:T(128)}, s3...) while((s32[]{:T(128)}, f32[8,4,128,128]{3,2,1,0:T(8,128)}, ...), condition=%wide.region_7.8_spmd, body=%wide.region_4.7_spmd.sunk | while | flops 187044160 | bytes 8235483 | solution.py:77
  (324 shorter events, 203.1 us)
Async XLA Ops:
  6.5 52.1 %all-gather.2.cloned.1.call-start = ((), (), s32[]{:S(2)}) async-start(), calls=%async_computation | async-start | bytes 3604480 | tf_op jit(solution)/shard_map/all_gather | solution.py:38
  7.3 71.2 %copy-start.2 = (s32[1024,11]{0,1:T(8,128)S(1)}, s32[1024,11]{0,1:T(8,128)}, u32[]{:S(2)}) copy-start(s32[1024,11]{0,1:T(8,128)} %param.9) | copy-start | bytes 135172
  7.3 72.3 %copy-start.3 = (s32[1024,12]{0,1:T(8,128)S(1)}, s32[1024,12]{0,1:T(8,128)}, u32[]{:S(2)}) copy-start(s32[1024,12]{0,1:T(8,128)} %param.10) | copy-start | bytes 147460
  63.0 382.1 %collective-permute-start = (bf16[5,11,128,128]{3,2,1,0:T(8,128)(2,1)}, bf16[5,11,128,128]{3,2,1,0:T(8,128)(2,1)}, u32[]{:S(2)}, u32[]{:S(2)}) collective-permute-start(bf16[5,11,128,128]{3,2,1,0:T(8,128)(2,1)} %get-tuple-element.390), channel_id=1, source_target_pairs={{0,1},{1,2},{2,3},{3,4},{4,5},{5,6},{6,7},{7,32},{32,33},{33,34},{... | collective-permute-start | bytes 5406728 | tf_op jit(solution)/shard_map/ppermute | solution.py:16
  74.9 372.2 %collective-permute-start.1 = (bf16[5,11,128,128]{3,2,1,0:T(8,128)(2,1)}, bf16[5,11,128,128]{3,2,1,0:T(8,128)(2,1)}, u32[]{:S(2)}, u32[]{:S(2)}) collective-permute-start(bf16[5,11,128,128]{3,2,1,0:T(8,128)(2,1)} %get-tuple-element.389), channel_id=1, source_target_pairs={{1,0},{2,1},{3,2},{4,3},{5,4},{6,5},{7,6},{32,7},{33,32},{34,33},{... | collective-permute-start | bytes 5406728 | tf_op jit(solution)/shard_map/ppermute | solution.py:17
  80.6 366.1 %copy-start.1 = (bf16[8,11,128,128]{3,2,1,0:T(8,128)(2,1)S(1)}, bf16[8,11,128,128]{3,2,1,0:T(8,128)(2,1)}, u32[]{:S(2)}) copy-start(bf16[8,11,128,128]{3,2,1,0:T(8,128)(2,1)} %all-gather.2.cloned.1.call-done) | copy-start | bytes 8650756
  448.9 2.7 copy-start
  732.8 18.1 %copy-start.4 = (s32[1024,16]{0,1:T(8,128)S(1)}, s32[1024,16]{0,1:T(8,128)}, u32[]{:S(2)}) copy-start(s32[1024,16]{0,1:T(8,128)} %param.11) | copy-start | bytes 196612
  735.4 332.2 %collective-permute-start.2 = (bf16[5,12,128,128]{3,2,1,0:T(8,128)(2,1)}, bf16[5,12,128,128]{3,2,1,0:T(8,128)(2,1)}, u32[]{:S(2)}, u32[]{:S(2)}) collective-permute-start(bf16[5,12,128,128]{3,2,1,0:T(8,128)(2,1)} %get-tuple-element.387), channel_id=1, source_target_pairs={{0,1},{1,2},{2,3},{3,4},{4,5},{5,6},{6,7},{7,32},{32,33},{33,34},{... | collective-permute-start | bytes 5898248 | tf_op jit(solution)/shard_map/ppermute | solution.py:16
  737.3 330.3 %collective-permute-start.3 = (bf16[5,12,128,128]{3,2,1,0:T(8,128)(2,1)}, bf16[5,12,128,128]{3,2,1,0:T(8,128)(2,1)}, u32[]{:S(2)}, u32[]{:S(2)}) collective-permute-start(bf16[5,12,128,128]{3,2,1,0:T(8,128)(2,1)} %get-tuple-element.388), channel_id=1, source_target_pairs={{1,0},{2,1},{3,2},{4,3},{5,4},{6,5},{7,6},{32,7},{33,32},{34,33},{... | collective-permute-start | bytes 5898248 | tf_op jit(solution)/shard_map/ppermute | solution.py:17
Sparse Core Ops, SparseCore 0:
  9.5 49.1 all-gather.1
where the time goes:
time: 1220 us
  waiting for transfers between devices  732 us (60%)
  local copies, waits for them, and re-layouts  303 us (25%)
  matrix products  53.8 us (4%)
  other arithmetic  52.6 us (4%)
  loops' own time  31.8 us (3%)
  starting transfers between devices  31 us (3%)
  between operations  13.6 us (1%)
    ppermute x2, waiting for transfers between devices, extended_2(): before = lax.ppermute(last, axis, up)  680 us
    gather x24, local copies, waits for them, and re-layouts, product_row(): picked = right_blocks[position[:, None], picked_slot]  204 us
    all_gather x1, waiting for transfers between devices, per_device(): whole_rows = lax.all_gather(density, 'col', axis=2, tiled=True)  51.3 us
    dot_general x16, matrix products, product_row(): jnp.einsum('axy,ajyz->jxz', left, picked, preferred_element_type=jnp.floa...  51.1 us
    gather x16, local copies, waits for them, and re-layouts, product_row(): right_listed = jnp.take(right_lists, source, axis=0)  25.6 us
  transfers between devices with their start and end apart: 5, of which 3 were waited for; matrix products, arithmetic and copies ran while one was open for 0% of the time, Pallas kernels for 0%

commit v1 on v0

v1 whole, which is shorter than its diff:
```python
import functools

import jax
import jax.numpy as jnp
from jax import lax
from jax.experimental import pallas as pl
from jax.experimental.pallas import tpu as pltpu
from jax.sharding import PartitionSpec as P

MESH = pl.DeviceIdType.MESH
RADIUS = 5
HALF = RADIUS + 1
BAND = 2 * RADIUS + 1
SQUARE_REACH = 2 * RADIUS
ROWS = 8
COLS = 4
BEFORE = 16
HELD = BEFORE + ROWS + 10
Z_CHUNKS = 2


def band_kernel(total_rows, first_row, pattern_ref, density_ref, upper_ref):
    upper_ref[...] = jnp.zeros_like(upper_ref)
    first = first_row[0]

    def row(i, carry):
        for s in range(density_ref.shape[1]):
            column = pattern_ref[i, s]
            offset = lax.rem(column - (first + i) + total_rows, total_rows)

            @pl.when((column >= 0) & (offset <= RADIUS))
            def _():
                upper_ref[i, offset] = density_ref[i, s]

        return carry

    lax.fori_loop(0, ROWS, row, 0)


def gather_kernel(upper_ref, held_ref, send, recv, local):
    row, col, layer = (lax.axis_index(a) for a in ("row", "col", "layer"))
    n_row, n_layer = lax.axis_size("row"), lax.axis_size("layer")
    side = lax.rem(layer, 2)
    up = lax.div(layer + 2, n_layer)
    down = 1 - lax.div(layer + n_layer - 2, n_layer)
    partner = {"layer": layer + 1 - 2 * side}
    after = {"row": lax.rem(row + up, n_row), "layer": lax.rem(layer + 2, n_layer)}
    before = {
        "row": lax.rem(row + n_row - down, n_row),
        "layer": lax.rem(layer + n_layer - 2, n_layer),
    }
    relay = {k: after[k] * (1 - side) + before[k] * side for k in after}
    right, left = lax.rem(col + 1, COLS), lax.rem(col + COLS - 1, COLS)

    barrier = pltpu.get_barrier_semaphore()
    for peer in (partner, after, before, {"col": left}, {"col": right}):
        pl.semaphore_signal(barrier, inc=1, device_id=peer, device_id_type=MESH)
    pl.semaphore_wait(barrier, 5)

    started = []

    def copy(src, dst, device):
        n = len(started)
        c = pltpu.make_async_remote_copy(
            src_ref=src,
            dst_ref=dst,
            send_sem=send.at[n],
            recv_sem=recv.at[n],
            device_id=device,
            device_id_type=MESH,
        )
        c.start()
        started.append(c)
        return c

    def spread(src, rows):
        return (
            copy(src, held_ref.at[col, rows], {"col": right}),
            copy(src, held_ref.at[col, rows], {"col": left}),
        )

    def forward(pair, rows):
        from_left, from_right = pair
        from_left.wait_recv()
        a = held_ref.at[left, rows, 0:3]
        to_right = copy(a, a, {"col": right})
        from_right.wait_recv()
        b = held_ref.at[right, rows, 3:HALF]
        to_left = copy(b, b, {"col": left})
        return to_right, to_left

    own = pl.ds(BEFORE, ROWS)
    keep = pltpu.make_async_copy(upper_ref, held_ref.at[col, own], local)
    keep.start()

    step = ROWS // Z_CHUNKS
    seen_as = 8 + 16 * side
    seen = 24 - 16 * side
    across = [
        copy(
            upper_ref.at[pl.ds(k * step, step)],
            held_ref.at[col, pl.ds(seen_as + k * step, step)],
            partner,
        )
        for k in range(Z_CHUNKS)
    ]
    own_pair = spread(upper_ref, own)
    far = pl.ds(1, ROWS - 1)
    far_copy = copy(upper_ref.at[far], held_ref.at[col, far], after)
    edge = pl.ds(BEFORE + 2 * ROWS, 2)
    edge_copy = copy(upper_ref.at[pl.ds(0, 2)], held_ref.at[col, edge], before)

    pending = []
    far_copy.wait_recv()
    far_pair = spread(held_ref.at[col, far], far)
    edge_copy.wait_recv()
    edge_pair = spread(held_ref.at[col, edge], edge)
    pending += forward(own_pair, own)
    relayed, pairs = [], []
    for k in range(Z_CHUNKS):
        across[k].wait_recv()
        got = pl.ds(seen + k * step, step)
        src = held_ref.at[col, got]
        put = pl.ds(seen_as + k * step, step)
        relayed.append((copy(src, held_ref.at[col, put], relay), put))
        pairs.append((spread(src, got), got))
    pending += forward(far_pair, far)
    pending += forward(edge_pair, edge)
    for c, rows in relayed:
        c.wait_recv()
        pairs.append((spread(held_ref.at[col, rows], rows), rows))
    for pair, rows in pairs:
        pending += forward(pair, rows)
    for c in pending:
        c.wait_recv()
    for c in started:
        c.wait_send()
    keep.wait()


N_COPIES = 2 + Z_CHUNKS * 2 + 4 * (3 + 2 * Z_CHUNKS)
BAND_ROWS = 39
SQUARE_ROWS = ROWS + 2 * RADIUS
SQUARE_COLUMNS = BAND_ROWS - 1


def product_kernel(
    total_rows, block, first_row, square_lists, targets, held_ref, out_ref, band, square, member, need
):
    first = first_row[0]
    offsets = 2 * SQUARE_REACH + 1

    def clear(k, carry):
        for e in range(offsets):
            member[k, e] = 0
            need[k, e] = 0
        return carry

    lax.fori_loop(0, SQUARE_ROWS, clear, 0)

    def listed(k, carry):
        for s in range(square_lists.shape[1]):
            e = lax.rem(
                square_lists[k, s] - (first + k - RADIUS) + SQUARE_REACH + 2 * total_rows,
                total_rows,
            )
            member[k, e] = 1
        return carry

    lax.fori_loop(0, SQUARE_ROWS, listed, 0)

    def place_of(i, t):
        return lax.rem(
            targets[i, t] - first + 3 * RADIUS + 2 * total_rows, total_rows
        )

    def wanted(i, carry):
        for t in range(targets.shape[1]):
            place = place_of(i, t)
            for q in range(BAND):
                k = i + q
                e = place - 3 * RADIUS - (k - RADIUS) + SQUARE_REACH
                inside = (e >= 0) & (e < offsets)
                hit = inside & (member[k, jnp.clip(e, 0, offsets - 1)] == 1)

                @pl.when(hit)
                def _():
                    need[k, e] = 1

                @pl.when(jnp.logical_not(hit))
                def _():
                    square[place, pl.ds(pl.multiple_of(k * block, block), block), :] = (
                        jnp.zeros((block, block), square.dtype)
                    )

        return carry

    lax.fori_loop(0, ROWS, wanted, 0)

    def unfold(a, carry):
        for d in range(HALF):
            whole = jnp.concatenate([held_ref[c, a, d] for c in range(COLS)], axis=0)

            @pl.when(a < BAND_ROWS)
            def _():
                band[a, :, (RADIUS + d) * block : (RADIUS + d + 1) * block] = whole

            if d > 0:

                @pl.when(a + d < BAND_ROWS)
                def _():
                    band[a + d, :, (RADIUS - d) * block : (RADIUS - d + 1) * block] = whole.T

        return carry

    lax.fori_loop(1, HELD, unfold, 0)

    def squares(k, carry):
        p = k + BEFORE - RADIUS
        for e in range(-SQUARE_REACH, SQUARE_REACH + 1):

            @pl.when(need[k, e + SQUARE_REACH] == 1)
            def _():
                width = (BAND - abs(e)) * block
                a, b = max(e, 0) * block, max(-e, 0) * block
                value = lax.dot_general(
                    band[p, :, a : a + width],
                    band[p + e, :, b : b + width],
                    (((1,), (1,)), ((), ())),
                    preferred_element_type=jnp.float32,
                )
                square[
                    p + e - 1, pl.ds(pl.multiple_of(k * block, block), block), :
                ] = value.astype(square.dtype)

        return carry

    lax.fori_loop(0, SQUARE_ROWS, squares, 0)

    def cubes(i, carry):
        left = band[i + BEFORE]
        rows = pl.ds(pl.multiple_of(i * block, block), BAND * block)
        mine = pl.ds(pl.multiple_of((i + RADIUS) * block, block), block)
        for t in range(0, targets.shape[1], 2):
            places = [place_of(i, t), place_of(i, t + 1)]
            right = jnp.concatenate([square[c, rows, :] for c in places], axis=1)
            cube = jnp.dot(left, right, preferred_element_type=jnp.float32)
            for n in range(2):
                own = square[places[n], mine, :].astype(jnp.float32)
                out_ref[i, t + n] = 3.0 * own - 2.0 * cube[:, n * block : (n + 1) * block]
        return carry

    lax.fori_loop(0, ROWS, cubes, 0)


def per_device(density, pattern, square_filter, cube_filter):
    n_layer = lax.axis_size("layer")
    total_rows = pattern.shape[0]
    rows, slots, part, block = density.shape
    first = (lax.axis_index("row") * n_layer + lax.axis_index("layer")) * ROWS
    first_row = first.astype(jnp.int32)[None]
    smem = pl.BlockSpec(memory_space=pltpu.SMEM)
    vmem = pl.BlockSpec(memory_space=pltpu.VMEM)
    anywhere = pl.BlockSpec(memory_space=pl.ANY)

    own_pattern = lax.dynamic_slice_in_dim(pattern, first, ROWS, 0)
    upper = pl.pallas_call(
        functools.partial(band_kernel, total_rows),
        out_shape=jax.ShapeDtypeStruct((ROWS, HALF, part, block), density.dtype),
        in_specs=[smem, smem, vmem],
        out_specs=vmem,
        name="band",
    )(first_row, own_pattern, density)

    held = pl.pallas_call(
        gather_kernel,
        out_shape=jax.ShapeDtypeStruct((COLS, HELD, HALF, part, block), density.dtype),
        in_specs=[anywhere],
        out_specs=anywhere,
        scratch_shapes=[
            pltpu.SemaphoreType.DMA((N_COPIES,)),
            pltpu.SemaphoreType.DMA((N_COPIES,)),
            pltpu.SemaphoreType.DMA,
        ],
        compiler_params=pltpu.CompilerParams(collective_id=0, has_side_effects=True),
        name="gather",
    )(upper)

    around = lax.rem(first - RADIUS + total_rows + jnp.arange(SQUARE_ROWS), total_rows)
    square_lists = jnp.take(square_filter, around, axis=0)
    share = cube_filter.shape[1] // COLS
    targets = lax.dynamic_slice(
        cube_filter, (first, lax.axis_index("col") * share), (ROWS, share)
    )
    return pl.pallas_call(
        functools.partial(product_kernel, total_rows, block),
        out_shape=jax.ShapeDtypeStruct((ROWS, share, block, block), jnp.float32),
        in_specs=[smem, smem, smem, vmem],
        out_specs=vmem,
        scratch_shapes=[
            pltpu.VMEM((BAND_ROWS, block, BAND * block), density.dtype),
            pltpu.VMEM((SQUARE_COLUMNS, SQUARE_ROWS * block, block), density.dtype),
            pltpu.SMEM((SQUARE_ROWS, 2 * SQUARE_REACH + 1), jnp.int32),
            pltpu.SMEM((SQUARE_ROWS, 2 * SQUARE_REACH + 1), jnp.int32),
        ],
        compiler_params=pltpu.CompilerParams(vmem_limit_bytes=60 << 20),
        name="product",
    )(first_row, square_lists, targets, held)


def solution(mesh):
    in_specs = (P(("row", "layer"), None, "col", None), P(), P(), P())
    out_specs = P(("row", "layer"), "col", None, None)
    return jax.shard_map(
        per_device, mesh=mesh, in_specs=in_specs, out_specs=out_specs, check_vma=False
    )
```

time: 1220 us -> 152 us (0.12)
  the two profiles are of different devices: /device:TPU:32 before, /device:TPU:34 now
where the time goes in v1:
time: 152 us
  Pallas kernels  147 us (97%)
  local copies, waits for them, and re-layouts  3.8 us (2%)
    pallas_call x1, Pallas kernels, per_device(): pl.pallas_call(gather_kernel, out_shape=jax.ShapeDtypeStruct((COLS, HELD,...  89.4 us
    pallas_call x1, Pallas kernels, per_device(): pl.pallas_call(functools.partial(product_kernel, total_rows, block), out_...  54.7 us
    pallas_call x1, Pallas kernels, per_device(): pl.pallas_call(functools.partial(band_kernel, total_rows), out_shape=jax....  3.12 us

profile of v1, /device:TPU:34, one launch (start us, length us, event | category | flops | bytes accessed | tf_op | source)
XLA Modules:
  0.0 151.8 jit_solution(9318792082769871651)
XLA Ops:
  0.0 0.0 copy-start
  0.0 0.8 dynamic_slice.6
  0.8 0.7 copy.8.targets
  1.5 0.0 copy-done
  1.5 0.1 constant_dynamic-slice_fusion
  1.6 0.7 copy.9.pattern_ref
  2.2 3.1 %band.1.upper_ref = bf16[8,6,32,128]{3,2,1,0:T(8,128)(2,1)} custom-call(s32[1]{0:T(128)} %bitcast.first_row, s32[8,11]{1,0:T(8,128)} %copy.9.pattern_ref, bf16[8,11,32,128]{3,2,1,0:T(8,128)(2,1)} %density_ref.1), custom_call_target="tpu_custom_call" | custom-call | tf_op jit(solution)/shard_map/band/pallas_call | solution.py:267
  5.3 1.0 copy.5
  6.4 0.6 gather_fusion
  7.0 0.7 broadcast_select_fusion.square_lists
  7.6 89.4 %gather.8.held_ref = bf16[4,34,6,32,128]{4,3,2,1,0:T(8,128)(2,1)} custom-call(bf16[8,6,32,128]{3,2,1,0:T(8,128)(2,1)} %band.1.upper_ref), custom_call_target="tpu_custom_call" | custom-call | tf_op jit(solution)/shard_map/gather/pallas_call | solution.py:275
  97.1 54.7 %product.1 = f32[8,4,128,128]{3,2,1,0:T(8,128)} custom-call(s32[1]{0:T(128)} %bitcast.first_row, s32[18,12]{1,0:T(8,128)} %broadcast_select_fusion.square_lists, s32[8,4]{1,0:T(8,128)} %copy.8.targets, bf16[4,34,6,32,128]{4,3,2,1,0:T(8,128)(2,1)} %gather.8.held_ref), custom_call_target="tpu_custom_call" | custom-call | tf_op jit(solution)/shard_map/product/pallas_call | solution.py:295
  (3 shorter events, 0.0 us)
Async XLA Ops:
  0.0 1.5 copy-start

commit v2 on v1

v2 whole, which is shorter than its diff:
```python
import jax
import jax.numpy as jnp
from jax import lax
from jax.experimental import pallas as pl
from jax.experimental.pallas import tpu as pltpu
from jax.sharding import PartitionSpec as P

MESH = pl.DeviceIdType.MESH
RADIUS = 5
HALF = RADIUS + 1
BAND = 2 * RADIUS + 1
SQUARE_REACH = 2 * RADIUS
ROWS = 8
COLS = 4
BEFORE = 16


def block_list():
    within = [(i, d) for d in range(HALF) for i in range(ROWS - d)]
    near = [(i, d) for i, d in within if i < 2]
    tail = [(i, d) for i, d in within if i + d >= ROWS - 2]
    lower = [(i, -d) for i in range(RADIUS) for d in range(i + 1, HALF)]
    early = [b for b in within if b not in near and b not in tail]
    upper = [(i, d) for d in range(1, HALF) for i in range(ROWS - d, ROWS)]
    both = [b for b in tail if b in near]
    near = [b for b in near if b not in both]
    tail = [b for b in tail if b not in both]
    return lower + early + near + both + tail + upper


OWN = block_list()
LOWER = slice(0, 15)
WITHIN = slice(15, 48)
EDGE = slice(25, 37)
FAR = slice(36, 63)
N_OWN = len(OWN)
AT_ACROSS = N_OWN
AT_RELAY = AT_ACROSS + 33
AT_FAR = AT_RELAY + 33
AT_LOWER = AT_FAR + 27
AT_EDGE = AT_LOWER + 15
HELD = AT_EDGE + 12


def gather_kernel(pattern, density_ref, band_ref, upper, held, send, recv):
    row, col, layer = (lax.axis_index(a) for a in ("row", "col", "layer"))
    n_row, n_layer = lax.axis_size("row"), lax.axis_size("layer")
    side = lax.rem(layer, 2)
    up = lax.div(layer + 2, n_layer)
    down = 1 - lax.div(layer + n_layer - 2, n_layer)
    partner = {"layer": layer + 1 - 2 * side}
    after = {"row": lax.rem(row + up, n_row), "layer": lax.rem(layer + 2, n_layer)}
    before = {
        "row": lax.rem(row + n_row - down, n_row),
        "layer": lax.rem(layer + n_layer - 2, n_layer),
    }
    relay = {k: after[k] * (1 - side) + before[k] * side for k in after}
    right, left = lax.rem(col + 1, COLS), lax.rem(col + COLS - 1, COLS)
    block = density_ref.shape[-1]

    barrier = pltpu.get_barrier_semaphore()
    for peer in (partner, after, before, {"col": left}, {"col": right}):
        pl.semaphore_signal(barrier, inc=1, device_id=peer, device_id_type=MESH)

    slots, total_rows = pattern.shape
    first = (row * n_layer + layer) * ROWS
    columns = [[pattern[s, first + i] for s in range(slots)] for i in range(ROWS)]
    for n, (i, d) in enumerate(OWN):
        target = lax.rem(first + i + d + total_rows, total_rows)
        slot = jnp.int32(-1)
        for s in range(slots):
            slot = jnp.where(columns[i][s] == target, s, slot)
        found = density_ref[i, jnp.maximum(slot, 0)]
        upper[n] = jnp.where(slot >= 0, found, jnp.zeros_like(found))

    pl.semaphore_wait(barrier, 5)

    started, waited = [], set()

    def copy(src, dst, device):
        n = len(started)
        c = pltpu.make_async_remote_copy(
            src_ref=src,
            dst_ref=dst,
            send_sem=send.at[n],
            recv_sem=recv.at[n],
            device_id=device,
            device_id_type=MESH,
        )
        c.start()
        started.append(c)
        return c

    def arrived(c):
        if id(c) not in waited:
            c.wait_recv()
            waited.add(id(c))

    def spread(src, at, n):
        rows = pl.ds(at, n)
        return (
            copy(src, held.at[col, rows], {"col": right}),
            copy(src, held.at[col, rows], {"col": left}),
        )

    def forward(pair, at, n):
        half = n // 2
        arrived(pair[0])
        a = held.at[left, pl.ds(at, half)]
        first = copy(a, a, {"col": right})
        arrived(pair[1])
        b = held.at[right, pl.ds(at + half, n - half)]
        return first, copy(b, b, {"col": left})

    def sideways(at, n, from_y):
        rows = pl.ds(at, n)
        arrived(from_y[0])
        a = held.at[col, rows]
        first = copy(a, a, {"col": left})
        arrived(from_y[1])
        b = held.at[left, rows]
        return first, copy(b, b, {"col": right})

    def place(whole, p, d):
        at = RADIUS + d
        band_ref[p, :, at * block : (at + 1) * block] = whole
        if d:
            at = RADIUS - d
            band_ref[p + d, :, at * block : (at + 1) * block] = whole.T

    def unfold(at, blocks, base, own=None):
        for n, (i, d) in enumerate(blocks):
            parts = [held[c, at + n] for c in range(COLS)]
            place(jnp.concatenate(parts, axis=0), base + i, d)

    pieces = 3
    size = 33 // pieces
    seen = 24 - 16 * side
    seen_as = 8 + 16 * side
    own_parts = ((36, 27), (0, 36))
    across = [
        copy(
            upper.at[pl.ds(WITHIN.start + k * size, size)],
            held.at[col, pl.ds(AT_ACROSS + k * size, size)],
            partner,
        )
        for k in range(pieces)
    ]
    own_pairs = [spread(upper.at[pl.ds(at, n)], at, n) for at, n in own_parts]
    groups = (
        (FAR, AT_FAR, after),
        (LOWER, AT_LOWER, before),
        (EDGE, AT_EDGE, before),
    )
    first_slices = [
        copy(upper.at[g], held.at[col, pl.ds(at, g.stop - g.start)], device)
        for g, at, device in groups
    ]
    held[col, 0:N_OWN] = upper[...]
    arrived(own_pairs[0][0])
    arrived(own_pairs[1][0])
    second_slices = [
        copy(held.at[left, g], held.at[left, pl.ds(at, g.stop - g.start)], device)
        for g, at, device in groups
    ]
    own_last = [forward(p, at, n) for p, (at, n) in zip(own_pairs, own_parts)]
    side_last = [
        sideways(at, g.stop - g.start, (a, b))
        for (g, at, _), a, b in zip(groups, first_slices, second_slices)
    ]

    across_pairs, relay_first, relay_second, across_last, relay_last = [], [], [], [], []

    def take_across(k):
        arrived(across[k])
        at, put = AT_ACROSS + k * size, AT_RELAY + k * size
        src = held.at[col, pl.ds(at, size)]
        relay_first.append(copy(src, held.at[col, pl.ds(put, size)], relay))
        across_pairs.append(spread(src, at, size))

    def pass_on(k):
        at, put = AT_ACROSS + k * size, AT_RELAY + k * size
        arrived(across_pairs[k][0])
        src = held.at[left, pl.ds(at, size)]
        relay_second.append(copy(src, held.at[left, pl.ds(put, size)], relay))
        across_last.append(forward(across_pairs[k], at, size))

    for k in range(pieces):
        take_across(k)
        if k:
            pass_on(k - 1)
    for c in own_last[0]:
        arrived(c)
    pass_on(pieces - 1)
    for c in own_last[1]:
        arrived(c)
    unfold(0, OWN, BEFORE)
    for k in range(pieces):
        relay_last.append(
            sideways(AT_RELAY + k * size, size, (relay_first[k], relay_second[k]))
        )
    bases = (0, BEFORE + 2 * ROWS, BEFORE + 2 * ROWS)
    for (g, at, _), last, base in zip(groups, side_last, bases):
        for c in last:
            arrived(c)
        unfold(at, OWN[g], base)
    for group, at0, base in ((across_last, AT_ACROSS, seen), (relay_last, AT_RELAY, seen_as)):
        for k, last in enumerate(group):
            for c in last:
                arrived(c)
            at = WITHIN.start + k * size
            unfold(at0 + k * size, OWN[at : at + size], base)
    for c in started:
        arrived(c)
        c.wait_send()


N_COPIES = 47
BAND_ROWS = 39
SQUARE_ROWS = ROWS + 2 * RADIUS
SQUARE_COLUMNS = BAND_ROWS - 1


def product_kernel(
    square_lists, cube_lists, band, out_ref, square, member, need
):
    n_layer = lax.axis_size("layer")
    first = (lax.axis_index("row") * n_layer + lax.axis_index("layer")) * ROWS
    share, block = out_ref.shape[1:3]
    first_target = lax.axis_index("col") * share
    total_rows = square_lists.shape[1]
    offsets = 2 * SQUARE_REACH + 1

    def clear(k, carry):
        for e in range(offsets):
            member[k, e] = 0
            need[k, e] = 0
        return carry

    lax.fori_loop(0, SQUARE_ROWS, clear, 0)

    def listed(k, carry):
        row = lax.rem(first + k - RADIUS + total_rows, total_rows)
        for s in range(square_lists.shape[0]):
            e = square_lists[s, row] - row + SQUARE_REACH + total_rows
            member[k, lax.rem(e, total_rows)] = 1
        return carry

    lax.fori_loop(0, SQUARE_ROWS, listed, 0)

    def place_of(i, t):
        return lax.rem(
            cube_lists[first_target + t, first + i] - first + 3 * RADIUS + total_rows, total_rows
        )

    def wanted(i, carry):
        for t in range(share):
            place = place_of(i, t)
            for q in range(BAND):
                k = i + q
                e = place - 3 * RADIUS - (k - RADIUS) + SQUARE_REACH
                inside = (e >= 0) & (e < offsets)
                hit = inside & (member[k, jnp.clip(e, 0, offsets - 1)] == 1)

                @pl.when(hit)
                def _():
                    need[k, e] = 1

                @pl.when(jnp.logical_not(hit))
                def _():
                    square[place, pl.ds(pl.multiple_of(k * block, block), block), :] = (
                        jnp.zeros((block, block), square.dtype)
                    )

        return carry

    lax.fori_loop(0, ROWS, wanted, 0)

    def squares(k, carry):
        p = k + BEFORE - RADIUS
        for e in range(-SQUARE_REACH, SQUARE_REACH + 1):

            @pl.when(need[k, e + SQUARE_REACH] == 1)
            def _():
                width = (BAND - abs(e)) * block
                a, b = max(e, 0) * block, max(-e, 0) * block
                value = lax.dot_general(
                    band[p, :, a : a + width],
                    band[p + e, :, b : b + width],
                    (((1,), (1,)), ((), ())),
                    preferred_element_type=jnp.float32,
                )
                square[
                    p + e - 1, pl.ds(pl.multiple_of(k * block, block), block), :
                ] = value.astype(square.dtype)

        return carry

    lax.fori_loop(0, SQUARE_ROWS, squares, 0)

    def cubes(i, carry):
        left = band[i + BEFORE]
        rows = pl.ds(pl.multiple_of(i * block, block), BAND * block)
        mine = pl.ds(pl.multiple_of((i + RADIUS) * block, block), block)
        for t in range(0, share, 2):
            places = [place_of(i, t), place_of(i, t + 1)]
            right = jnp.concatenate([square[c, rows, :] for c in places], axis=1)
            cube = jnp.dot(left, right, preferred_element_type=jnp.float32)
            for n in range(2):
                own = square[places[n], mine, :].astype(jnp.float32)
                out_ref[i, t + n] = 3.0 * own - 2.0 * cube[:, n * block : (n + 1) * block]
        return carry

    lax.fori_loop(0, ROWS, cubes, 0)


def per_device(density, pattern, square_filter, cube_filter):
    part, block = density.shape[2:]
    share = cube_filter.shape[1] // COLS
    smem = pl.BlockSpec(memory_space=pltpu.SMEM)
    vmem = pl.BlockSpec(memory_space=pltpu.VMEM)

    band = pl.pallas_call(
        gather_kernel,
        out_shape=jax.ShapeDtypeStruct((BAND_ROWS, block, BAND * block), density.dtype),
        in_specs=[smem, vmem],
        out_specs=vmem,
        scratch_shapes=[
            pltpu.VMEM((N_OWN, part, block), density.dtype),
            pltpu.VMEM((COLS, HELD, part, block), density.dtype),
            pltpu.SemaphoreType.DMA((N_COPIES,)),
            pltpu.SemaphoreType.DMA((N_COPIES,)),
        ],
        compiler_params=pltpu.CompilerParams(
            collective_id=0, has_side_effects=True, vmem_limit_bytes=24 << 20
        ),
        name="gather",
    )(pattern.T, density)

    return pl.pallas_call(
        product_kernel,
        out_shape=jax.ShapeDtypeStruct((ROWS, share, block, block), jnp.float32),
        in_specs=[smem, smem, vmem],
        out_specs=vmem,
        scratch_shapes=[
            pltpu.VMEM((SQUARE_COLUMNS, SQUARE_ROWS * block, block), density.dtype),
            pltpu.SMEM((SQUARE_ROWS, 2 * SQUARE_REACH + 1), jnp.int32),
            pltpu.SMEM((SQUARE_ROWS, 2 * SQUARE_REACH + 1), jnp.int32),
        ],
        compiler_params=pltpu.CompilerParams(vmem_limit_bytes=28 << 20),
        name="product",
    )(square_filter.T, cube_filter.T, band)


def solution(mesh):
    in_specs = (P(("row", "layer"), None, "col", None), P(), P(), P())
    out_specs = P(("row", "layer"), "col", None, None)
    return jax.shard_map(
        per_device, mesh=mesh, in_specs=in_specs, out_specs=out_specs, check_vma=False
    )
```

time: 152 us -> 116 us (0.76)
  the two profiles are of different devices: /device:TPU:34 before, /device:TPU:6 now
where the time goes in v2:
time: 116 us
  Pallas kernels  114 us (98%)
  local copies, waits for them, and re-layouts  1.96 us (2%)
    pallas_call x1, Pallas kernels, per_device(): pl.pallas_call(gather_kernel, out_shape=jax.ShapeDtypeStruct((BAND_ROWS,...  72.4 us
    pallas_call x1, Pallas kernels, per_device(): pl.pallas_call(product_kernel, out_shape=jax.ShapeDtypeStruct((ROWS, shar...  41.8 us

profile of v2, /device:TPU:6, one launch (start us, length us, event | category | flops | bytes accessed | tf_op | source)
XLA Modules:
  0.0 116.2 jit_solution(6058194878907650375)
XLA Ops:
  0.0 0.0 copy-start
  0.0 1.1 copy-done
  1.1 0.0 copy-start.1
  1.1 0.8 copy-done.1
  2.0 0.0 copy-start.2
  2.0 0.0 copy-start.3
  2.0 72.4 %gather.1.band = bf16[39,128,1408]{2,1,0:T(8,128)(2,1)S(1)} custom-call(s32[11,1024]{1,0:T(8,128)S(1)} %bitcast.3, bf16[8,11,32,128]{3,2,1,0:T(8,128)(2,1)S(1)} %copy-done), custom_call_target="tpu_custom_call" | custom-call | tf_op jit(solution)/shard_map/gather/pallas_call | solution.py:323
  74.3 0.0 copy-done.2
  74.4 0.0 copy-done.3
  74.4 41.8 %product.1 = f32[8,4,128,128]{3,2,1,0:T(8,128)} custom-call(s32[12,1024]{1,0:T(8,128)S(1)} %bitcast.4, s32[16,1024]{1,0:T(8,128)S(1)} %bitcast.5, bf16[39,128,1408]{2,1,0:T(8,128)(2,1)S(1)} %gather.1.band), custom_call_target="tpu_custom_call" | custom-call | tf_op jit(solution)/shard_map/product/pallas_call | solution.py:340
Async XLA Ops:
  0.0 1.1 copy-start
  1.1 0.8 copy-start.1
  2.0 72.4 %copy-start.2 = (s32[1024,12]{0,1:T(8,128)S(1)}, s32[1024,12]{0,1:T(8,128)}, u32[]{:S(2)}) copy-start(s32[1024,12]{0,1:T(8,128)} %param.6) | copy-start | bytes 147460
  2.0 72.4 %copy-start.3 = (s32[1024,16]{0,1:T(8,128)S(1)}, s32[1024,16]{0,1:T(8,128)}, u32[]{:S(2)}) copy-start(s32[1024,16]{0,1:T(8,128)} %param.7) | copy-start | bytes 196612

commit v3 on v2

--- a/solution.py
+++ b/solution.py
@@ -121,22 +121,23 @@
         b = held.at[left, rows]
         return first, copy(b, b, {"col": right})
 
-    def place(whole, p, d):
-        at = RADIUS + d
-        band_ref[p, :, at * block : (at + 1) * block] = whole
-        if d:
-            at = RADIUS - d
-            band_ref[p + d, :, at * block : (at + 1) * block] = whole.T
-
-    def unfold(at, blocks, base, own=None):
+    def place(whole, base, p, d):
+        lane = (p % 2 + RADIUS + d) * block
+        row = p % 2 * block
+        band_ref[base + p // 2, row : row + block, lane : lane + block] = whole
+
+    def unfold(at, blocks, base):
         for n, (i, d) in enumerate(blocks):
             parts = [held[c, at + n] for c in range(COLS)]
-            place(jnp.concatenate(parts, axis=0), base + i, d)
+            whole = jnp.concatenate(parts, axis=0)
+            place(whole, base, i, d)
+            if d:
+                place(whole.T, base, i + d, -d)
 
     pieces = 3
     size = 33 // pieces
-    seen = 24 - 16 * side
-    seen_as = 8 + 16 * side
+    seen = 12 - 8 * side
+    seen_as = 4 + 8 * side
     own_parts = ((36, 27), (0, 36))
     across = [
         copy(
@@ -157,6 +158,13 @@
         for g, at, device in groups
     ]
     held[col, 0:N_OWN] = upper[...]
+    for n in range(BAND_PAIRS):
+        if 5 <= n < 15:
+            corner = jnp.zeros((block, block), band_ref.dtype)
+            band_ref[n, 0:block, BAND * block :] = corner
+            band_ref[n, block:, 0:block] = corner
+        else:
+            band_ref[n] = jnp.zeros_like(band_ref[n])
     arrived(own_pairs[0][0])
     arrived(own_pairs[1][0])
     second_slices = [
@@ -194,12 +202,12 @@
     pass_on(pieces - 1)
     for c in own_last[1]:
         arrived(c)
-    unfold(0, OWN, BEFORE)
+    unfold(0, OWN, BEFORE // 2)
     for k in range(pieces):
         relay_last.append(
             sideways(AT_RELAY + k * size, size, (relay_first[k], relay_second[k]))
         )
-    bases = (0, BEFORE + 2 * ROWS, BEFORE + 2 * ROWS)
+    bases = (0, BEFORE // 2 + ROWS, BEFORE // 2 + ROWS)
     for (g, at, _), last, base in zip(groups, side_last, bases):
         for c in last:
             arrived(c)
@@ -216,102 +224,81 @@
 
 
 N_COPIES = 47
-BAND_ROWS = 39
-SQUARE_ROWS = ROWS + 2 * RADIUS
-SQUARE_COLUMNS = BAND_ROWS - 1
-
-
-def product_kernel(
-    square_lists, cube_lists, band, out_ref, square, member, need
-):
+BAND_PAIRS = 20
+SQUARE_PAIRS = 10
+WIDTH = BAND + 1
+
+
+def product_kernel(square_lists, cube_lists, band, out_ref, square, member):
     n_layer = lax.axis_size("layer")
     first = (lax.axis_index("row") * n_layer + lax.axis_index("layer")) * ROWS
     share, block = out_ref.shape[1:3]
     first_target = lax.axis_index("col") * share
     total_rows = square_lists.shape[1]
-    offsets = 2 * SQUARE_REACH + 1
-
-    def clear(k, carry):
-        for e in range(offsets):
+    reach = SQUARE_REACH + 1
+
+    def listed(k, carry):
+        for e in range(2 * reach + 1):
             member[k, e] = 0
-            need[k, e] = 0
-        return carry
-
-    lax.fori_loop(0, SQUARE_ROWS, clear, 0)
-
-    def listed(k, carry):
-        row = lax.rem(first + k - RADIUS + total_rows, total_rows)
+        row = lax.rem(first + k - RADIUS - 1 + total_rows, total_rows)
         for s in range(square_lists.shape[0]):
-            e = square_lists[s, row] - row + SQUARE_REACH + total_rows
+            e = square_lists[s, row] - row + reach + total_rows
             member[k, lax.rem(e, total_rows)] = 1
         return carry
 
-    lax.fori_loop(0, SQUARE_ROWS, listed, 0)
-
-    def place_of(i, t):
-        return lax.rem(
-            cube_lists[first_target + t, first + i] - first + 3 * RADIUS + total_rows, total_rows
-        )
-
-    def wanted(i, carry):
-        for t in range(share):
-            place = place_of(i, t)
-            for q in range(BAND):
-                k = i + q
-                e = place - 3 * RADIUS - (k - RADIUS) + SQUARE_REACH
-                inside = (e >= 0) & (e < offsets)
-                hit = inside & (member[k, jnp.clip(e, 0, offsets - 1)] == 1)
-
-                @pl.when(hit)
-                def _():
-                    need[k, e] = 1
-
-                @pl.when(jnp.logical_not(hit))
-                def _():
-                    square[place, pl.ds(pl.multiple_of(k * block, block), block), :] = (
-                        jnp.zeros((block, block), square.dtype)
+    lax.fori_loop(0, 2 * SQUARE_PAIRS, listed, 0)
+
+    for j in range(BAND_PAIRS):
+        for k in range(SQUARE_PAIRS):
+            if abs(j - k - 5) > RADIUS:
+                for h in range(2):
+                    square[2 * j + h, 2 * k * block : 2 * (k + 1) * block, :] = jnp.zeros(
+                        (2 * block, block), square.dtype
                     )
 
+    def squares(k, carry):
+        for e in range(-RADIUS, RADIUS + 1):
+            width = (WIDTH - 2 * abs(e)) * block
+            a, b = max(2 * e, 0) * block, max(-2 * e, 0) * block
+            value = lax.dot_general(
+                band[k + 5, :, a : a + width],
+                band[k + 5 + e, :, b : b + width],
+                (((1,), (1,)), ((), ())),
+                preferred_element_type=jnp.float32,
+            )
+            for hj in range(2):
+                for hk in range(2):
+                    kept = member[2 * k + hk, 2 * e + hj - hk + reach] == 1
+                    part = value[hk * block : (hk + 1) * block, hj * block : (hj + 1) * block]
+                    row = pl.multiple_of((2 * k + hk) * block, block)
+                    square[2 * (k + 5 + e) + hj, pl.ds(row, block), :] = jnp.where(
+                        kept, part, 0.0
+                    ).astype(square.dtype)
         return carry
 
-    lax.fori_loop(0, ROWS, wanted, 0)
-
-    def squares(k, carry):
-        p = k + BEFORE - RADIUS
-        for e in range(-SQUARE_REACH, SQUARE_REACH + 1):
-
-            @pl.when(need[k, e + SQUARE_REACH] == 1)
-            def _():
-                width = (BAND - abs(e)) * block
-                a, b = max(e, 0) * block, max(-e, 0) * block
-                value = lax.dot_general(
-                    band[p, :, a : a + width],
-                    band[p + e, :, b : b + width],
-                    (((1,), (1,)), ((), ())),
-                    preferred_element_type=jnp.float32,
+    lax.fori_loop(0, SQUARE_PAIRS, squares, 0)
+
+    def cubes(n, carry):
+        for h in range(2):
+            i = 2 * n + h
+            left = band[n + BEFORE // 2, h * block : (h + 1) * block, h * block : (h + BAND) * block]
+            rows = pl.ds(pl.multiple_of((i + 1) * block, block), BAND * block)
+            mine = pl.ds(pl.multiple_of((i + 1 + RADIUS) * block, block), block)
+            places = [
+                lax.rem(
+                    cube_lists[first_target + t, first + i] - first + BEFORE + total_rows,
+                    total_rows,
                 )
-                square[
-                    p + e - 1, pl.ds(pl.multiple_of(k * block, block), block), :
-                ] = value.astype(square.dtype)
-
-        return carry
-
-    lax.fori_loop(0, SQUARE_ROWS, squares, 0)
-
-    def cubes(i, carry):
-        left = band[i + BEFORE]
-        rows = pl.ds(pl.multiple_of(i * block, block), BAND * block)
-        mine = pl.ds(pl.multiple_of((i + RADIUS) * block, block), block)
-        for t in range(0, share, 2):
-            places = [place_of(i, t), place_of(i, t + 1)]
+                for t in range(share)
+            ]
             right = jnp.concatenate([square[c, rows, :] for c in places], axis=1)
             cube = jnp.dot(left, right, preferred_element_type=jnp.float32)
-            for n in range(2):
-                own = square[places[n], mine, :].astype(jnp.float32)
-                out_ref[i, t + n] = 3.0 * own - 2.0 * cube[:, n * block : (n + 1) * block]
+            for t, c in enumerate(places):
+                own = square[c, mine, :].astype(jnp.float32)
+                out_ref[i, t] = 3.0 * own - 2.0 * cube[:, t * block : (t + 1) * block]
         return carry
 
-    lax.fori_loop(0, ROWS, cubes, 0)
+    lax.fori_loop(0, ROWS // 2, cubes, 0)
 
 
 def per_device(density, pattern, square_filter, cube_filter):
@@ -322,7 +309,7 @@
 
     band = pl.pallas_call(
         gather_kernel,
-        out_shape=jax.ShapeDtypeStruct((BAND_ROWS, block, BAND * block), density.dtype),
+        out_shape=jax.ShapeDtypeStruct((BAND_PAIRS, 2 * block, WIDTH * block), density.dtype),
         in_specs=[smem, vmem],
         out_specs=vmem,
         scratch_shapes=[
@@ -343,11 +330,10 @@
         in_specs=[smem, smem, vmem],
         out_specs=vmem,
         scratch_shapes=[
-            pltpu.VMEM((SQUARE_COLUMNS, SQUARE_ROWS * block, block), density.dtype),
-            pltpu.SMEM((SQUARE_ROWS, 2 * SQUARE_REACH + 1), jnp.int32),
-            pltpu.SMEM((SQUARE_ROWS, 2 * SQUARE_REACH + 1), jnp.int32),
+            pltpu.VMEM((2 * BAND_PAIRS, 2 * SQUARE_PAIRS * block, block), density.dtype),
+            pltpu.SMEM((2 * SQUARE_PAIRS, 2 * SQUARE_REACH + 3), jnp.int32),
         ],
-        compiler_params=pltpu.CompilerParams(vmem_limit_bytes=28 << 20),
+        compiler_params=pltpu.CompilerParams(vmem_limit_bytes=31 << 20),
         name="product",
     )(square_filter.T, cube_filter.T, band)
 

time: 116 us -> 98.9 us (0.85)
  Pallas kernels: 114 us -> 96.3 us
    pallas_call x1, Pallas kernels: 41.8 us -> 23.9 us  [per_device(): pl.pallas_call(product_kernel, out_shape=jax.ShapeDtypeStruct((ROWS, shar...]
where the time goes in v3:
time: 98.9 us; the launch traced here: 98.3 us
  Pallas kernels  96.3 us (97%)
  local copies, waits for them, and re-layouts  1.96 us (2%)
    pallas_call x1, Pallas kernels, per_device(): pl.pallas_call(gather_kernel, out_shape=jax.ShapeDtypeStruct((BAND_PAIRS,...  72.4 us
    pallas_call x1, Pallas kernels, per_device(): pl.pallas_call(product_kernel, out_shape=jax.ShapeDtypeStruct((ROWS, shar...  23.9 us

profile of v3, /device:TPU:6, one launch (start us, length us, event | category | flops | bytes accessed | tf_op | source)
XLA Modules:
  0.0 98.3 jit_solution(9311876740681805620)
XLA Ops:
  0.0 0.0 copy-start
  0.0 1.1 %copy-done = bf16[8,11,32,128]{3,2,1,0:T(8,128)(2,1)S(1)} copy-done((bf16[8,11,32,128]{3,2,1,0:T(8,128)(2,1)S(1)}, bf16[8,11,32,128]{3,2,1,0:T(8,128)(2,1)}, u32[]{:S(2)}) %copy-start) | copy-done | bytes 720920
  1.1 0.0 copy-start.1
  1.1 0.8 copy-done.1
  2.0 0.0 copy-start.2
  2.0 0.0 copy-start.3
  2.0 72.4 %gather.1.band = bf16[20,256,1536]{2,1,0:T(8,128)(2,1)S(1)} custom-call(s32[11,1024]{1,0:T(8,128)S(1)} %bitcast.3, bf16[8,11,32,128]{3,2,1,0:T(8,128)(2,1)S(1)} %copy-done), custom_call_target="tpu_custom_call" | custom-call | tf_op jit(solution)/shard_map/gather/pallas_call | solution.py:310
  74.3 0.0 copy-done.2
  74.4 0.0 copy-done.3
  74.4 23.9 %product.1 = f32[8,4,128,128]{3,2,1,0:T(8,128)} custom-call(s32[12,1024]{1,0:T(8,128)S(1)} %bitcast.4, s32[16,1024]{1,0:T(8,128)S(1)} %bitcast.5, bf16[20,256,1536]{2,1,0:T(8,128)(2,1)S(1)} %gather.1.band), custom_call_target="tpu_custom_call" | custom-call | tf_op jit(solution)/shard_map/product/pallas_call | solution.py:327
Async XLA Ops:
  0.0 1.1 %copy-start = (bf16[8,11,32,128]{3,2,1,0:T(8,128)(2,1)S(1)}, bf16[8,11,32,128]{3,2,1,0:T(8,128)(2,1)}, u32[]{:S(2)}) copy-start(bf16[8,11,32,128]{3,2,1,0:T(8,128)(2,1)} %density_ref.1) | copy-start | bytes 2162692
  1.1 0.8 copy-start.1
  2.0 72.4 %copy-start.2 = (s32[1024,12]{0,1:T(8,128)S(1)}, s32[1024,12]{0,1:T(8,128)}, u32[]{:S(2)}) copy-start(s32[1024,12]{0,1:T(8,128)} %param.6) | copy-start | bytes 147460
  2.0 72.4 %copy-start.3 = (s32[1024,16]{0,1:T(8,128)S(1)}, s32[1024,16]{0,1:T(8,128)}, u32[]{:S(2)}) copy-start(s32[1024,16]{0,1:T(8,128)} %param.7) | copy-start | bytes 196612

commit v4 on v3

--- a/solution.py
+++ b/solution.py
@@ -13,6 +13,11 @@
 ROWS = 8
 COLS = 4
 BEFORE = 16
+
+
+BAND_PAIRS = 20
+SQUARE_PAIRS = 10
+WIDTH = BAND + 1
 
 
 def block_list():
@@ -42,7 +47,20 @@
 HELD = AT_EDGE + 12
 
 
-def gather_kernel(pattern, density_ref, band_ref, upper, held, send, recv):
+def purify_kernel(
+    pattern,
+    square_lists,
+    cube_lists,
+    density_ref,
+    out_ref,
+    band_ref,
+    square,
+    upper,
+    held,
+    member,
+    send,
+    recv,
+):
     row, col, layer = (lax.axis_index(a) for a in ("row", "col", "layer"))
     n_row, n_layer = lax.axis_size("row"), lax.axis_size("layer")
     side = lax.rem(layer, 2)
@@ -64,15 +82,18 @@
 
     slots, total_rows = pattern.shape
     first = (row * n_layer + layer) * ROWS
-    columns = [[pattern[s, first + i] for s in range(slots)] for i in range(ROWS)]
-    for n, (i, d) in enumerate(OWN):
-        target = lax.rem(first + i + d + total_rows, total_rows)
-        slot = jnp.int32(-1)
-        for s in range(slots):
-            slot = jnp.where(columns[i][s] == target, s, slot)
-        found = density_ref[i, jnp.maximum(slot, 0)]
-        upper[n] = jnp.where(slot >= 0, found, jnp.zeros_like(found))
-
+
+    def take_own(blocks):
+        for n in range(blocks.start, blocks.stop):
+            i, d = OWN[n]
+            target = lax.rem(first + i + d + total_rows, total_rows)
+            slot = jnp.int32(-1)
+            for s in range(slots):
+                slot = jnp.where(pattern[s, first + i] == target, s, slot)
+            found = density_ref[i, jnp.maximum(slot, 0)]
+            upper[n] = jnp.where(slot >= 0, found, jnp.zeros_like(found))
+
+    take_own(WITHIN)
     pl.semaphore_wait(barrier, 5)
 
     started, waited = [], set()
@@ -147,6 +168,8 @@
         )
         for k in range(pieces)
     ]
+    take_own(slice(WITHIN.stop, N_OWN))
+    take_own(LOWER)
     own_pairs = [spread(upper.at[pl.ds(at, n)], at, n) for at, n in own_parts]
     groups = (
         (FAR, AT_FAR, after),
@@ -165,6 +188,51 @@
             band_ref[n, block:, 0:block] = corner
         else:
             band_ref[n] = jnp.zeros_like(band_ref[n])
+    for j in range(BAND_PAIRS):
+        for k in range(SQUARE_PAIRS):
+            if abs(j - k - 5) > RADIUS:
+                for h in range(2):
+                    square[2 * j + h, 2 * k * block : 2 * (k + 1) * block, :] = jnp.zeros(
+                        (2 * block, block), square.dtype
+                    )
+    reach = SQUARE_REACH + 1
+
+    def table(k, carry):
+        at = lax.rem(first + k - RADIUS - 1 + total_rows, total_rows)
+        listed = [square_lists[s, at] for s in range(square_lists.shape[0])]
+        for e in range(2 * reach + 1):
+            target = lax.rem(at + e - reach + total_rows, total_rows)
+            kept = jnp.int32(0)
+            for one in listed:
+                kept = jnp.where(one == target, 1, kept)
+            member[k, e] = kept
+        return carry
+
+    lax.fori_loop(0, 2 * SQUARE_PAIRS, table, 0)
+
+    def square_pair(k, e):
+        width = (WIDTH - 2 * abs(e)) * block
+        a, b = max(2 * e, 0) * block, max(-2 * e, 0) * block
+        value = lax.dot_general(
+            band_ref[k, :, a : a + width],
+            band_ref[k + e, :, b : b + width],
+            (((1,), (1,)), ((), ())),
+            preferred_element_type=jnp.float32,
+        )
+        for hj in range(2):
+            for hk in range(2):
+                at = 2 * (k - 5) + hk
+                kept = member[at, 2 * e + hj - hk + reach] == 1
+                part = value[hk * block : (hk + 1) * block, hj * block : (hj + 1) * block]
+                rows = pl.ds(pl.multiple_of(at * block, block), block)
+                square[2 * (k + e) + hj, rows, :] = jnp.where(kept, part, 0.0).astype(
+                    square.dtype
+                )
+
+    def square_rows(k, carry):
+        for e in range(-RADIUS, RADIUS + 1):
+            square_pair(k, e)
+        return carry
     arrived(own_pairs[0][0])
     arrived(own_pairs[1][0])
     second_slices = [
@@ -199,95 +267,57 @@
             pass_on(k - 1)
     for c in own_last[0]:
         arrived(c)
-    pass_on(pieces - 1)
     for c in own_last[1]:
         arrived(c)
-    unfold(0, OWN, BEFORE // 2)
-    for k in range(pieces):
-        relay_last.append(
-            sideways(AT_RELAY + k * size, size, (relay_first[k], relay_second[k]))
-        )
-    bases = (0, BEFORE // 2 + ROWS, BEFORE // 2 + ROWS)
-    for (g, at, _), last, base in zip(groups, side_last, bases):
+    unfold(0, OWN[0:36], BEFORE // 2)
+    pass_on(pieces - 1)
+    unfold(36, OWN[36:], BEFORE // 2)
+
+    def unfold_piece(at0, k, last, base):
         for c in last:
             arrived(c)
-        unfold(at, OWN[g], base)
-    for group, at0, base in ((across_last, AT_ACROSS, seen), (relay_last, AT_RELAY, seen_as)):
-        for k, last in enumerate(group):
-            for c in last:
-                arrived(c)
-            at = WITHIN.start + k * size
-            unfold(at0 + k * size, OWN[at : at + size], base)
-    for c in started:
-        arrived(c)
-        c.wait_send()
-
-
-N_COPIES = 47
-BAND_PAIRS = 20
-SQUARE_PAIRS = 10
-WIDTH = BAND + 1
-
-
-def product_kernel(square_lists, cube_lists, band, out_ref, square, member):
-    n_layer = lax.axis_size("layer")
-    first = (lax.axis_index("row") * n_layer + lax.axis_index("layer")) * ROWS
-    share, block = out_ref.shape[1:3]
-    first_target = lax.axis_index("col") * share
-    total_rows = square_lists.shape[1]
-    reach = SQUARE_REACH + 1
-
-    def listed(k, carry):
-        for e in range(2 * reach + 1):
-            member[k, e] = 0
-        row = lax.rem(first + k - RADIUS - 1 + total_rows, total_rows)
-        for s in range(square_lists.shape[0]):
-            e = square_lists[s, row] - row + reach + total_rows
-            member[k, lax.rem(e, total_rows)] = 1
-        return carry
-
-    lax.fori_loop(0, 2 * SQUARE_PAIRS, listed, 0)
-
-    for j in range(BAND_PAIRS):
-        for k in range(SQUARE_PAIRS):
-            if abs(j - k - 5) > RADIUS:
-                for h in range(2):
-                    square[2 * j + h, 2 * k * block : 2 * (k + 1) * block, :] = jnp.zeros(
-                        (2 * block, block), square.dtype
-                    )
-
-    def squares(k, carry):
-        for e in range(-RADIUS, RADIUS + 1):
-            width = (WIDTH - 2 * abs(e)) * block
-            a, b = max(2 * e, 0) * block, max(-2 * e, 0) * block
-            value = lax.dot_general(
-                band[k + 5, :, a : a + width],
-                band[k + 5 + e, :, b : b + width],
-                (((1,), (1,)), ((), ())),
-                preferred_element_type=jnp.float32,
-            )
-            for hj in range(2):
-                for hk in range(2):
-                    kept = member[2 * k + hk, 2 * e + hj - hk + reach] == 1
-                    part = value[hk * block : (hk + 1) * block, hj * block : (hj + 1) * block]
-                    row = pl.multiple_of((2 * k + hk) * block, block)
-                    square[2 * (k + 5 + e) + hj, pl.ds(row, block), :] = jnp.where(
-                        kept, part, 0.0
-                    ).astype(square.dtype)
-        return carry
-
-    lax.fori_loop(0, SQUARE_PAIRS, squares, 0)
+        at = WITHIN.start + k * size
+        unfold(at0 + k * size, OWN[at : at + size], base)
+
+    bases = (0, BEFORE // 2 + ROWS, BEFORE // 2 + ROWS)
+    for k in range(pieces):
+        at = AT_RELAY + k * size
+        relay_last.append(sideways(at, size, (relay_first[k], relay_second[k])))
+        g, at, _ = groups[k]
+        for c in side_last[k]:
+            arrived(c)
+        unfold(at, OWN[g], bases[k])
+    for k in range(pieces):
+        unfold_piece(AT_ACROSS, k, across_last[k], seen)
+
+    lax.fori_loop(8 - 3 * side, 15 - 3 * side, square_rows, 0)
+    for k in range(pieces):
+        unfold_piece(AT_RELAY, k, relay_last[k], seen_as)
+    lax.fori_loop(5 + 7 * side, 8 + 7 * side, square_rows, 0)
+    again = [(k, j) for k in range(8, 13) for j in range(max(4, k - RADIUS), 8)]
+    for which in range(2):
+
+        @pl.when(side == which)
+        def _():
+            for k, j in again:
+                square_pair(19 - k if which else k, k - j if which else j - k)
+
+    share = out_ref.shape[1]
+    first_target = col * share
 
     def cubes(n, carry):
         for h in range(2):
             i = 2 * n + h
-            left = band[n + BEFORE // 2, h * block : (h + 1) * block, h * block : (h + BAND) * block]
+            left = band_ref[n + BEFORE // 2, h * block : (h + 1) * block, h * block : (h + BAND) * block]
             rows = pl.ds(pl.multiple_of((i + 1) * block, block), BAND * block)
             mine = pl.ds(pl.multiple_of((i + 1 + RADIUS) * block, block), block)
             places = [
-                lax.rem(
-                    cube_lists[first_target + t, first + i] - first + BEFORE + total_rows,
-                    total_rows,
+                jnp.minimum(
+                    lax.rem(
+                        cube_lists[first_target + t, first + i] - first + BEFORE + total_rows,
+                        total_rows,
+                    ),
+                    2 * BAND_PAIRS - 1,
                 )
                 for t in range(share)
             ]
@@ -300,42 +330,37 @@
 
     lax.fori_loop(0, ROWS // 2, cubes, 0)
 
-
+    for c in started:
+        arrived(c)
+        c.wait_send()
+
+
+N_COPIES = 47
 def per_device(density, pattern, square_filter, cube_filter):
     part, block = density.shape[2:]
     share = cube_filter.shape[1] // COLS
     smem = pl.BlockSpec(memory_space=pltpu.SMEM)
     vmem = pl.BlockSpec(memory_space=pltpu.VMEM)
 
-    band = pl.pallas_call(
-        gather_kernel,
-        out_shape=jax.ShapeDtypeStruct((BAND_PAIRS, 2 * block, WIDTH * block), density.dtype),
-        in_specs=[smem, vmem],
+    return pl.pallas_call(
+        purify_kernel,
+        out_shape=jax.ShapeDtypeStruct((ROWS, share, block, block), jnp.float32),
+        in_specs=[smem, smem, smem, vmem],
         out_specs=vmem,
         scratch_shapes=[
+            pltpu.VMEM((BAND_PAIRS, 2 * block, WIDTH * block), density.dtype),
+            pltpu.VMEM((2 * BAND_PAIRS, 2 * SQUARE_PAIRS * block, block), density.dtype),
             pltpu.VMEM((N_OWN, part, block), density.dtype),
             pltpu.VMEM((COLS, HELD, part, block), density.dtype),
+            pltpu.SMEM((2 * SQUARE_PAIRS, 2 * SQUARE_REACH + 3), jnp.int32),
             pltpu.SemaphoreType.DMA((N_COPIES,)),
             pltpu.SemaphoreType.DMA((N_COPIES,)),
         ],
         compiler_params=pltpu.CompilerParams(
-            collective_id=0, has_side_effects=True, vmem_limit_bytes=24 << 20
+            collective_id=0, has_side_effects=True, vmem_limit_bytes=54 << 20
         ),
-        name="gather",
-    )(pattern.T, density)
-
-    return pl.pallas_call(
-        product_kernel,
-        out_shape=jax.ShapeDtypeStruct((ROWS, share, block, block), jnp.float32),
-        in_specs=[smem, smem, vmem],
-        out_specs=vmem,
-        scratch_shapes=[
-            pltpu.VMEM((2 * BAND_PAIRS, 2 * SQUARE_PAIRS * block, block), density.dtype),
-            pltpu.SMEM((2 * SQUARE_PAIRS, 2 * SQUARE_REACH + 3), jnp.int32),
-        ],
-        compiler_params=pltpu.CompilerParams(vmem_limit_bytes=31 << 20),
-        name="product",
-    )(square_filter.T, cube_filter.T, band)
+        name="purify",
+    )(pattern.T, square_filter.T, cube_filter.T, density)
 
 
 def solution(mesh):

time: 98.9 us -> 95.6 us (0.967)
  Pallas kernels: 96.3 us -> 91.4 us
  local copies, waits for them, and re-layouts: 1.96 us -> 3.14 us
    pallas_call x2 -> x1, Pallas kernels: 96.3 us -> 91.4 us  [per_device(): pl.pallas_call(purify_kernel, out_shape=jax.ShapeDtypeStruct((ROWS, share...]
    unnamed x8 -> x1, local copies, waits for them, and re-layouts: 1.96 us -> 3.14 us
where the time goes in v4:
time: 95.6 us; the launch traced here: 94.5 us
  Pallas kernels  91.4 us (96%)
  local copies, waits for them, and re-layouts  3.14 us (3%)
    pallas_call x1, Pallas kernels, per_device(): pl.pallas_call(purify_kernel, out_shape=jax.ShapeDtypeStruct((ROWS, share...  91.4 us
    unnamed x1, local copies, waits for them, and re-layouts  3.14 us

profile of v4, /device:TPU:6, one launch (start us, length us, event | category | flops | bytes accessed | tf_op | source)
XLA Modules:
  0.0 94.5 jit_solution(351226525507451840)
XLA Ops:
  0.0 91.4 %purify.1 = f32[8,4,128,128]{3,2,1,0:T(8,128)} custom-call(s32[11,1024]{1,0:T(8,128)} %bitcast.3, s32[12,1024]{1,0:T(8,128)} %bitcast.4, s32[16,1024]{1,0:T(8,128)} %bitcast.5, bf16[8,11,32,128]{3,2,1,0:T(8,128)(2,1)} %density_ref.1), custom_call_target="tpu_custom_call" | custom-call | tf_op jit(solution)/shard_map/purify/pallas_call | solution.py:345
  91.4 3.1 %copy.6 = f32[8,4,128,128]{3,2,1,0:T(8,128)} copy(f32[8,4,128,128]{3,2,1,0:T(8,128)} %purify.1) | data formatting | bytes 4194304

commit v5 on v4

--- a/solution.py
+++ b/solution.py
@@ -181,20 +181,25 @@
         for g, at, device in groups
     ]
     held[col, 0:N_OWN] = upper[...]
-    for n in range(BAND_PAIRS):
-        if 5 <= n < 15:
-            corner = jnp.zeros((block, block), band_ref.dtype)
-            band_ref[n, 0:block, BAND * block :] = corner
-            band_ref[n, block:, 0:block] = corner
-        else:
-            band_ref[n] = jnp.zeros_like(band_ref[n])
-    for j in range(BAND_PAIRS):
-        for k in range(SQUARE_PAIRS):
-            if abs(j - k - 5) > RADIUS:
-                for h in range(2):
-                    square[2 * j + h, 2 * k * block : 2 * (k + 1) * block, :] = jnp.zeros(
-                        (2 * block, block), square.dtype
-                    )
+
+    def zero_band():
+        for n in range(BAND_PAIRS):
+            if 5 <= n < 15:
+                corner = jnp.zeros((block, block), band_ref.dtype)
+                band_ref[n, 0:block, BAND * block :] = corner
+                band_ref[n, block:, 0:block] = corner
+            else:
+                band_ref[n] = jnp.zeros_like(band_ref[n])
+
+    def zero_square():
+        for j in range(BAND_PAIRS):
+            for k in range(SQUARE_PAIRS):
+                if abs(j - k - 5) > RADIUS:
+                    for h in range(2):
+                        square[2 * j + h, 2 * k * block : 2 * (k + 1) * block, :] = jnp.zeros(
+                            (2 * block, block), square.dtype
+                        )
+
     reach = SQUARE_REACH + 1
 
     def table(k, carry):
@@ -208,42 +213,51 @@
             member[k, e] = kept
         return carry
 
-    lax.fori_loop(0, 2 * SQUARE_PAIRS, table, 0)
-
-    def square_pair(k, e):
+    def square_pair(k, j, e, a, b):
         width = (WIDTH - 2 * abs(e)) * block
-        a, b = max(2 * e, 0) * block, max(-2 * e, 0) * block
+        turned = (j - k) * 2 + reach
         value = lax.dot_general(
-            band_ref[k, :, a : a + width],
-            band_ref[k + e, :, b : b + width],
+            band_ref[k, :, pl.ds(pl.multiple_of(a, block), width)],
+            band_ref[j, :, pl.ds(pl.multiple_of(b, block), width)],
             (((1,), (1,)), ((), ())),
             preferred_element_type=jnp.float32,
         )
         for hj in range(2):
             for hk in range(2):
                 at = 2 * (k - 5) + hk
-                kept = member[at, 2 * e + hj - hk + reach] == 1
+                kept = member[at, turned + hj - hk] == 1
                 part = value[hk * block : (hk + 1) * block, hj * block : (hj + 1) * block]
                 rows = pl.ds(pl.multiple_of(at * block, block), block)
-                square[2 * (k + e) + hj, rows, :] = jnp.where(kept, part, 0.0).astype(
-                    square.dtype
-                )
+                square[2 * j + hj, rows, :] = jnp.where(kept, part, 0.0).astype(square.dtype)
+
+    def straight(k, e):
+        square_pair(k, k + e, e, max(2 * e, 0) * block, max(-2 * e, 0) * block)
 
     def square_rows(k, carry):
         for e in range(-RADIUS, RADIUS + 1):
-            square_pair(k, e)
+            straight(k, e)
         return carry
+
+    def mirrored(k, j):
+        e = j - k
+        a, b = max(2 * e, 0) * block, max(-2 * e, 0) * block
+        square_pair(
+            k + side * (19 - 2 * k), j + side * (19 - 2 * j), e, a + side * (b - a), b + side * (a - b)
+        )
+
+    zero_band()
     arrived(own_pairs[0][0])
+
+    def second(n):
+        g, at, device = groups[n]
+        return copy(held.at[left, g], held.at[left, pl.ds(at, g.stop - g.start)], device)
+
+    second_slices = [second(0)]
+    lax.fori_loop(0, 2 * SQUARE_PAIRS, table, 0)
     arrived(own_pairs[1][0])
-    second_slices = [
-        copy(held.at[left, g], held.at[left, pl.ds(at, g.stop - g.start)], device)
-        for g, at, device in groups
-    ]
+    second_slices += [second(1), second(2)]
     own_last = [forward(p, at, n) for p, (at, n) in zip(own_pairs, own_parts)]
-    side_last = [
-        sideways(at, g.stop - g.start, (a, b))
-        for (g, at, _), a, b in zip(groups, first_slices, second_slices)
-    ]
+    zero_square()
 
     across_pairs, relay_first, relay_second, across_last, relay_last = [], [], [], [], []
 
@@ -261,46 +275,54 @@
         relay_second.append(copy(src, held.at[left, pl.ds(put, size)], relay))
         across_last.append(forward(across_pairs[k], at, size))
 
-    for k in range(pieces):
-        take_across(k)
-        if k:
-            pass_on(k - 1)
-    for c in own_last[0]:
-        arrived(c)
-    for c in own_last[1]:
-        arrived(c)
-    unfold(0, OWN[0:36], BEFORE // 2)
-    pass_on(pieces - 1)
-    unfold(36, OWN[36:], BEFORE // 2)
-
     def unfold_piece(at0, k, last, base):
         for c in last:
             arrived(c)
         at = WITHIN.start + k * size
         unfold(at0 + k * size, OWN[at : at + size], base)
 
+    take_across(0)
+    for n in range(2):
+        at, count = own_parts[n]
+        for c in own_last[n]:
+            arrived(c)
+        unfold(at, OWN[at : at + count], BEFORE // 2)
+    take_across(1)
+    pass_on(0)
+    side_last = [
+        sideways(at, g.stop - g.start, (a, b))
+        for (g, at, _), a, b in zip(groups, first_slices, second_slices)
+    ]
+
+    for k in range(8, 12):
+        for j in range(8, 12):
+            straight(k, j - k)
+
+    take_across(2)
+    pass_on(1)
+    pass_on(2)
     bases = (0, BEFORE // 2 + ROWS, BEFORE // 2 + ROWS)
     for k in range(pieces):
-        at = AT_RELAY + k * size
-        relay_last.append(sideways(at, size, (relay_first[k], relay_second[k])))
         g, at, _ = groups[k]
         for c in side_last[k]:
             arrived(c)
         unfold(at, OWN[g], bases[k])
+        at = AT_RELAY + k * size
+        relay_last.append(sideways(at, size, (relay_first[k], relay_second[k])))
     for k in range(pieces):
         unfold_piece(AT_ACROSS, k, across_last[k], seen)
 
-    lax.fori_loop(8 - 3 * side, 15 - 3 * side, square_rows, 0)
+    lax.fori_loop(12 - 7 * side, 15 - 7 * side, square_rows, 0)
+    for k in range(8, 12):
+        for j in range(k - RADIUS, k + RADIUS + 1):
+            if not 4 <= j < 12:
+                mirrored(k, j)
     for k in range(pieces):
         unfold_piece(AT_RELAY, k, relay_last[k], seen_as)
     lax.fori_loop(5 + 7 * side, 8 + 7 * side, square_rows, 0)
-    again = [(k, j) for k in range(8, 13) for j in range(max(4, k - RADIUS), 8)]
-    for which in range(2):
-
-        @pl.when(side == which)
-        def _():
-            for k, j in again:
-                square_pair(19 - k if which else k, k - j if which else j - k)
+    for k in range(8, 13):
+        for j in range(max(4, k - RADIUS), 8):
+            mirrored(k, j)
 
     share = out_ref.shape[1]
     first_target = col * share
@@ -357,7 +379,7 @@
             pltpu.SemaphoreType.DMA((N_COPIES,)),
         ],
         compiler_params=pltpu.CompilerParams(
-            collective_id=0, has_side_effects=True, vmem_limit_bytes=54 << 20
+            collective_id=0, has_side_effects=True, vmem_limit_bytes=50 << 20
         ),
         name="purify",
     )(pattern.T, square_filter.T, cube_filter.T, density)

time: 95.6 us -> 90.1 us (0.942)
  the two profiles are of different devices: /device:TPU:6 before, /device:TPU:72 now
where the time goes in v5:
time: 90.1 us; the launch traced here: 89.9 us
  Pallas kernels  84.9 us (94%)
  local copies, waits for them, and re-layouts  4.95 us (5%)
    pallas_call x1, Pallas kernels, per_device(): pl.pallas_call(purify_kernel, out_shape=jax.ShapeDtypeStruct((ROWS, share...  84.9 us
    unnamed x9, local copies, waits for them, and re-layouts  4.95 us

profile of v5, /device:TPU:72, one launch (start us, length us, event | category | flops | bytes accessed | tf_op | source)
XLA Modules:
  0.0 89.9 jit_solution(17007925202994977135)
XLA Ops:
  0.0 0.0 copy-start
  0.0 1.1 %copy-done = bf16[8,11,32,128]{3,2,1,0:T(8,128)(2,1)S(1)} copy-done((bf16[8,11,32,128]{3,2,1,0:T(8,128)(2,1)S(1)}, bf16[8,11,32,128]{3,2,1,0:T(8,128)(2,1)}, u32[]{:S(2)}) %copy-start) | copy-done | bytes 720920
  1.1 0.0 copy-start.1
  1.1 0.8 copy-done.1
  2.0 0.0 copy-start.2
  2.0 0.8 copy-done.2
  2.8 0.0 copy-start.3
  2.8 0.8 copy-done.3
  3.6 84.9 %purify.1 = f32[8,4,128,128]{3,2,1,0:T(8,128)S(1)} custom-call(s32[11,1024]{1,0:T(8,128)S(1)} %bitcast.3, s32[12,1024]{1,0:T(8,128)S(1)} %bitcast.4, s32[16,1024]{1,0:T(8,128)S(1)} %bitcast.5, bf16[8,11,32,128]{3,2,1,0:T(8,128)(2,1)S(1)} %copy-done), custom_call_target="tpu_custom_call" | custom-call | tf_op jit(solution)/shard_map/purify/pallas_call | solution.py:367
  88.5 1.3 %copy.6 = f32[8,4,128,128]{3,2,1,0:T(8,128)} copy(f32[8,4,128,128]{3,2,1,0:T(8,128)S(1)} %purify.1) | data formatting | bytes 4194304
Async XLA Ops:
  0.0 1.1 %copy-start = (bf16[8,11,32,128]{3,2,1,0:T(8,128)(2,1)S(1)}, bf16[8,11,32,128]{3,2,1,0:T(8,128)(2,1)}, u32[]{:S(2)}) copy-start(bf16[8,11,32,128]{3,2,1,0:T(8,128)(2,1)} %density_ref.1) | copy-start | bytes 2162692
  1.1 0.8 copy-start.1
  2.0 0.8 copy-start.2
  2.8 0.8 copy-start.3

commit v6 on v5

--- a/solution.py
+++ b/solution.py
@@ -1,3 +1,5 @@
+import functools
+
 import jax
 import jax.numpy as jnp
 from jax import lax
@@ -48,16 +50,21 @@
 
 
 def purify_kernel(
-    pattern,
-    square_lists,
-    cube_lists,
-    density_ref,
+    pattern_hbm,
+    square_lists_hbm,
+    cube_lists_hbm,
+    density_hbm,
     out_ref,
     band_ref,
     square,
     upper,
     held,
     member,
+    pattern,
+    square_lists,
+    cube_lists,
+    density_ref,
+    load,
     send,
     recv,
 ):
@@ -80,6 +87,21 @@
     for peer in (partner, after, before, {"col": left}, {"col": right}):
         pl.semaphore_signal(barrier, inc=1, device_id=peer, device_id_type=MESH)
 
+    loads = [
+        pltpu.make_async_copy(src, dst, load.at[n])
+        for n, (src, dst) in enumerate(
+            (
+                (pattern_hbm, pattern),
+                (density_hbm, density_ref),
+                (square_lists_hbm, square_lists),
+                (cube_lists_hbm, cube_lists),
+            )
+        )
+    ]
+    for one in loads:
+        one.start()
+    loads[0].wait()
+    loads[1].wait()
     slots, total_rows = pattern.shape
     first = (row * n_layer + layer) * ROWS
 
@@ -98,7 +120,7 @@
 
     started, waited = [], set()
 
-    def copy(src, dst, device):
+    def copy(src, dst, device, start=True):
         n = len(started)
         c = pltpu.make_async_remote_copy(
             src_ref=src,
@@ -108,7 +130,8 @@
             device_id=device,
             device_id_type=MESH,
         )
-        c.start()
+        if start:
+            c.start()
         started.append(c)
         return c
 
@@ -133,14 +156,19 @@
         b = held.at[right, pl.ds(at + half, n - half)]
         return first, copy(b, b, {"col": left})
 
-    def sideways(at, n, from_y):
+    def sideways(at, n, from_y, start=True):
         rows = pl.ds(at, n)
-        arrived(from_y[0])
-        a = held.at[col, rows]
-        first = copy(a, a, {"col": left})
-        arrived(from_y[1])
-        b = held.at[left, rows]
-        return first, copy(b, b, {"col": right})
+        a, b = held.at[col, rows], held.at[left, rows]
+        pair = copy(a, a, {"col": left}, False), copy(b, b, {"col": right}, False)
+        if start:
+            go_sideways(pair, from_y)
+        return pair
+
+    def go_sideways(pair, from_y):
+        for c, source in zip(pair, from_y):
+            source.wait_recv()
+            waited.add(id(source))
+            c.start()
 
     def place(whole, base, p, d):
         lane = (p % 2 + RADIUS + d) * block
@@ -246,6 +274,8 @@
         )
 
     zero_band()
+    loads[2].wait()
+    loads[3].wait()
     arrived(own_pairs[0][0])
 
     def second(n):
@@ -257,6 +287,26 @@
     arrived(own_pairs[1][0])
     second_slices += [second(1), second(2)]
     own_last = [forward(p, at, n) for p, (at, n) in zip(own_pairs, own_parts)]
+    side_last = [
+        sideways(at, g.stop - g.start, None, False) for g, at, _ in groups
+    ]
+    far_late = (layer < 2) & (lax.rem(row, 2) == 0)
+    near_late = (layer >= n_layer - 2) & (lax.rem(row, 2) == 1)
+    late = (far_late, near_late, near_late)
+    bases = (0, BEFORE // 2 + ROWS, BEFORE // 2 + ROWS)
+
+    def take_side(n):
+        go_sideways(side_last[n], (first_slices[n], second_slices[n]))
+
+    def unfold_side(n):
+        g, at, _ = groups[n]
+        for c in side_last[n]:
+            c.wait_recv()
+            waited.add(id(c))
+        unfold(at, OWN[g], bases[n])
+
+    for n in range(3):
+        pl.when(jnp.logical_not(late[n]))(functools.partial(take_side, n))
     zero_square()
 
     across_pairs, relay_first, relay_second, across_last, relay_last = [], [], [], [], []
@@ -289,24 +339,21 @@
         unfold(at, OWN[at : at + count], BEFORE // 2)
     take_across(1)
     pass_on(0)
-    side_last = [
-        sideways(at, g.stop - g.start, (a, b))
-        for (g, at, _), a, b in zip(groups, first_slices, second_slices)
-    ]
+    for n in range(3):
+        pl.when(late[n])(functools.partial(take_side, n))
 
     for k in range(8, 12):
         for j in range(8, 12):
             straight(k, j - k)
 
+    for n in range(3):
+        pl.when(jnp.logical_not(late[n]))(functools.partial(unfold_side, n))
     take_across(2)
     pass_on(1)
     pass_on(2)
-    bases = (0, BEFORE // 2 + ROWS, BEFORE // 2 + ROWS)
+    for n in range(3):
+        pl.when(late[n])(functools.partial(unfold_side, n))
     for k in range(pieces):
-        g, at, _ = groups[k]
-        for c in side_last[k]:
-            arrived(c)
-        unfold(at, OWN[g], bases[k])
         at = AT_RELAY + k * size
         relay_last.append(sideways(at, size, (relay_first[k], relay_second[k])))
     for k in range(pieces):
@@ -361,13 +408,13 @@
 def per_device(density, pattern, square_filter, cube_filter):
     part, block = density.shape[2:]
     share = cube_filter.shape[1] // COLS
-    smem = pl.BlockSpec(memory_space=pltpu.SMEM)
+    hbm = pl.BlockSpec(memory_space=pltpu.HBM)
     vmem = pl.BlockSpec(memory_space=pltpu.VMEM)
 
     return pl.pallas_call(
         purify_kernel,
         out_shape=jax.ShapeDtypeStruct((ROWS, share, block, block), jnp.float32),
-        in_specs=[smem, smem, smem, vmem],
+        in_specs=[hbm] * 4,
         out_specs=vmem,
         scratch_shapes=[
             pltpu.VMEM((BAND_PAIRS, 2 * block, WIDTH * block), density.dtype),
@@ -375,11 +422,16 @@
             pltpu.VMEM((N_OWN, part, block), density.dtype),
             pltpu.VMEM((COLS, HELD, part, block), density.dtype),
             pltpu.SMEM((2 * SQUARE_PAIRS, 2 * SQUARE_REACH + 3), jnp.int32),
+            pltpu.SMEM(pattern.shape[::-1], jnp.int32),
+            pltpu.SMEM(square_filter.shape[::-1], jnp.int32),
+            pltpu.SMEM(cube_filter.shape[::-1], jnp.int32),
+            pltpu.VMEM((ROWS, *density.shape[1:]), density.dtype),
+            pltpu.SemaphoreType.DMA((4,)),
             pltpu.SemaphoreType.DMA((N_COPIES,)),
             pltpu.SemaphoreType.DMA((N_COPIES,)),
         ],
         compiler_params=pltpu.CompilerParams(
-            collective_id=0, has_side_effects=True, vmem_limit_bytes=50 << 20
+            collective_id=0, has_side_effects=True, vmem_limit_bytes=60 << 20
         ),
         name="purify",
     )(pattern.T, square_filter.T, cube_filter.T, density)

time: 90.1 us -> 85.1 us (0.945)
  the two profiles are of different devices: /device:TPU:72 before, /device:TPU:1 now
where the time goes in v6:
time: 85.1 us; the launch traced here: 84.9 us
  Pallas kernels  81.7 us (96%)
  local copies, waits for them, and re-layouts  3.14 us (4%)
    pallas_call x1, Pallas kernels, per_device(): pl.pallas_call(purify_kernel, out_shape=jax.ShapeDtypeStruct((ROWS, share...  81.7 us
    unnamed x1, local copies, waits for them, and re-layouts  3.14 us

profile of v6, /device:TPU:1, one launch (start us, length us, event | category | flops | bytes accessed | tf_op | source)
XLA Modules:
  0.0 84.9 jit_solution(5390328878002209568)
XLA Ops:
  0.0 81.7 %purify.1 = f32[8,4,128,128]{3,2,1,0:T(8,128)} custom-call(s32[11,1024]{1,0:T(8,128)} %bitcast.3, s32[12,1024]{1,0:T(8,128)} %bitcast.4, s32[16,1024]{1,0:T(8,128)} %bitcast.5, bf16[8,11,32,128]{3,2,1,0:T(8,128)(2,1)} %density_hbm.1), custom_call_target="tpu_custom_call" | custom-call | tf_op jit(solution)/shard_map/purify/pallas_call | solution.py:414
  81.8 3.1 %copy.6 = f32[8,4,128,128]{3,2,1,0:T(8,128)} copy(f32[8,4,128,128]{3,2,1,0:T(8,128)} %purify.1) | data formatting | bytes 4194304

commit v7 on v6

--- a/solution.py
+++ b/solution.py
@@ -354,10 +354,12 @@
     for n in range(3):
         pl.when(late[n])(functools.partial(unfold_side, n))
     for k in range(pieces):
+        if k == pieces - 1:
+            unfold_piece(AT_ACROSS, k, across_last[k], seen)
         at = AT_RELAY + k * size
         relay_last.append(sideways(at, size, (relay_first[k], relay_second[k])))
-    for k in range(pieces):
-        unfold_piece(AT_ACROSS, k, across_last[k], seen)
+        if k < pieces - 1:
+            unfold_piece(AT_ACROSS, k, across_last[k], seen)
 
     lax.fori_loop(12 - 7 * side, 15 - 7 * side, square_rows, 0)
     for k in range(8, 12):

time: 85.1 us -> 84.3 us (level)
  no operation moved by 1% of the time
where the time goes in v7:
time: 84.3 us; the launch traced here: 84.1 us
  Pallas kernels  81 us (96%)
  local copies, waits for them, and re-layouts  3.14 us (4%)
    pallas_call x1, Pallas kernels, per_device(): pl.pallas_call(purify_kernel, out_shape=jax.ShapeDtypeStruct((ROWS, share...  81 us
    unnamed x1, local copies, waits for them, and re-layouts  3.14 us

profile of v7, /device:TPU:1, one launch (start us, length us, event | category | flops | bytes accessed | tf_op | source)
XLA Modules:
  0.0 84.1 jit_solution(16292794613707803307)
XLA Ops:
  0.0 81.0 %purify.1 = f32[8,4,128,128]{3,2,1,0:T(8,128)} custom-call(s32[11,1024]{1,0:T(8,128)} %bitcast.3, s32[12,1024]{1,0:T(8,128)} %bitcast.4, s32[16,1024]{1,0:T(8,128)} %bitcast.5, bf16[8,11,32,128]{3,2,1,0:T(8,128)(2,1)} %density_hbm.1), custom_call_target="tpu_custom_call" | custom-call | tf_op jit(solution)/shard_map/purify/pallas_call | solution.py:416
  81.0 3.1 %copy.6 = f32[8,4,128,128]{3,2,1,0:T(8,128)} copy(f32[8,4,128,128]{3,2,1,0:T(8,128)} %purify.1) | data formatting | bytes 4194304
